TPU v7x, 256 devices: a whole 4x4x8 slice. The times are simulated.
256 devices in a mesh: dst: 32 (over y, z), src: 8 (over x, core).
Axes of the slice: x: 4, y: 4, z: 8, core: 2. Of those that a mesh axis runs over, the one named last changes fastest.
Arguments:
- features: bfloat16 [131072, 128], P(('src', 'dst')), may hold values from -64 to 64
- projection: bfloat16 [128, 256], replicated, may hold values from -1 to 1
- source_att: float32 [256], replicated, may hold values from -1.5 to 1.5
- target_att: float32 [256], replicated, may hold values from -1 to 1
- out_bias: float32 [256], replicated, may hold values from -3 to 3
- block_coords: int32 [32, 8, 2, 256], P('dst', 'src'), may hold values from 0 to 127, as said below
- block_words: int32 [32, 8, 256, 16, 128], P('dst', 'src'), may hold values from 0 to 255, as said below
- block_counts: int32 [32, 8], P('dst', 'src'), may hold values from 1 to 256, as said below
Outputs:
- result: bfloat16 [131072, 256], P(('dst', 'src'))
Inputs may be any that keep to these rules, and one draw needn't show every extreme that they name: `block_coords`: row entries are below 32 and column entries below 128; the (row, column) pairs of one device's slots are distinct. `block_counts`: at least one device has all 256 slots live. `block_words`: each word holds an 8-bit pattern.
All inputs are finite; a program needn't handle non-finite values.
Results may differ from a plain program's by a relative error of at most 0.019.
Values may be sent and summed in bfloat16 or wider, within the bound.
No kernel may reach another device: no remote copies, remote signals or barrier semaphores. Data moves between devices by JAX's collectives and lax.ppermute only.
A program may use at most 128 MiB of HBM per device.

v0:
```python
import math
import jax
import jax.numpy as jnp
from jax import lax
from jax.sharding import PartitionSpec as P

HEADS = 8
HEAD_DIM = 32


def from_root(block, axis, holder):
    block = jnp.where(lax.axis_index(axis) == holder, block, jnp.zeros_like(block))
    return lax.psum(block, axis)


def leaky_relu(inputs):
    return jnp.where(inputs > 0, inputs, 0.2 * inputs)


def unpack(packed):
    shifts = jnp.arange(8, dtype=jnp.int32)
    spread = jnp.right_shift(packed[..., :, None, :], shifts[:, None]) & 1
    leading = packed.shape[:-2]
    flattened = spread.reshape(leading + (128, 128))
    return jnp.swapaxes(flattened, -1, -2) > 0


def terms_of(projected, source_att, target_att):
    source_part = jnp.sum(
        (projected * source_att).reshape(projected.shape[0], HEADS, HEAD_DIM), axis=-1
    )
    target_part = jnp.sum(
        (projected * target_att).reshape(projected.shape[0], HEADS, HEAD_DIM), axis=-1
    )
    return jnp.concatenate([source_part, target_part], axis=1).T


def on_device(
    features, projection, source_att, target_att, out_bias, block_coords, block_words, block_counts
):
    dst_count = lax.axis_size("dst")
    src_count = lax.axis_size("src")
    group_ratio = dst_count // src_count
    dst_index = lax.axis_index("dst")
    src_index = lax.axis_index("src")
    root_index = dst_index // group_ratio
    own_rows = features.shape[0]
    rows_dst = own_rows * src_count
    feature_width = projection.shape[1]
    projected = jnp.dot(features, projection, preferred_element_type=jnp.float32)
    gathered, score_terms = (
        lax.all_gather(projected.astype(jnp.bfloat16), "dst", axis=0, tiled=True),
        lax.all_gather(
            terms_of(projected, source_att, target_att).astype(jnp.bfloat16),
            "dst",
            axis=1,
            tiled=True,
        ).astype(jnp.float32),
    )
    src_rows = gathered.shape[0]
    row_blocks = rows_dst // 128
    col_blocks = src_rows // 128
    offset = dst_index % group_ratio * rows_dst
    target_own = lax.dynamic_slice_in_dim(score_terms[HEADS:], offset, rows_dst, 1)
    target_rows = from_root(target_own.astype(jnp.bfloat16), "src", root_index).astype(
        target_own.dtype
    )
    target_blocks = target_rows.reshape(HEADS, row_blocks, 128).transpose(1, 0, 2)
    source_blocks = score_terms[:HEADS].reshape(HEADS, col_blocks, 128).transpose(1, 0, 2)
    value_blocks = gathered.reshape(col_blocks, 128, HEADS, HEAD_DIM)
    self_source = (
        lax.dynamic_slice_in_dim(score_terms[:HEADS], offset, rows_dst, 1)
        .reshape(HEADS, row_blocks, 128)
        .transpose(1, 0, 2)
    )
    self_score = leaky_relu(target_blocks + self_source)
    is_root = src_index == root_index
    coords = block_coords[0, 0]
    packed_words = block_words[0, 0]
    live_count = block_counts[0, 0]
    group_size = math.gcd(packed_words.shape[0], 16)
    steps_live = (live_count + group_size - 1) // group_size

    def group_scores(step_index):
        first_slot = step_index * group_size
        row_ids = lax.dynamic_slice_in_dim(coords[0], first_slot, group_size)
        col_ids = lax.dynamic_slice_in_dim(coords[1], first_slot, group_size)
        packed = lax.dynamic_slice_in_dim(packed_words, first_slot, group_size, 0)
        valid_slot = first_slot + jnp.arange(group_size, dtype=jnp.int32) < live_count
        edge_mask = unpack(packed) & valid_slot[:, None, None]
        scores = leaky_relu(
            target_blocks[row_ids][:, :, :, None] + source_blocks[col_ids][:, :, None, :]
        )
        return (row_ids, col_ids, edge_mask, scores)

    def max_step(step_index, maxima):
        row_ids, col_ids, edge_mask, scores = group_scores(step_index)
        block_max = jnp.max(jnp.where(edge_mask[:, None], scores, -jnp.inf), axis=3)
        return maxima.at[row_ids].max(block_max)

    maxima = lax.fori_loop(
        0, steps_live, max_step, jnp.full((row_blocks, HEADS, 128), -jnp.inf, jnp.float32)
    )
    maxima = jnp.where(is_root, jnp.maximum(maxima, self_score), maxima)
    maxima = lax.pmax(maxima.astype(jnp.bfloat16), "src").astype(maxima.dtype)

    def sum_step(step_index, carry_state):
        weighted, denominator = carry_state
        row_ids, col_ids, edge_mask, scores = group_scores(step_index)
        weight = jnp.where(edge_mask[:, None], jnp.exp(scores - maxima[row_ids][..., None]), 0.0)
        rounded = weight.astype(jnp.bfloat16)
        contrib = jnp.einsum(
            "ghab,gbhc->gahc", rounded, value_blocks[col_ids], preferred_element_type=jnp.float32
        )
        contrib = contrib.reshape(group_size, 128, feature_width)
        weighted = weighted.at[row_ids].add(contrib)
        denominator = denominator.at[row_ids].add(jnp.sum(weight, axis=3))
        return (weighted, denominator)

    start_state = (
        jnp.zeros((row_blocks, 128, feature_width), jnp.float32),
        jnp.zeros((row_blocks, HEADS, 128), jnp.float32),
    )
    weighted, denominator = lax.fori_loop(0, steps_live, sum_step, start_state)
    self_weight = jnp.where(is_root, jnp.exp(self_score - maxima), 0.0)
    denominator = denominator + self_weight
    self_values = lax.dynamic_slice_in_dim(gathered, offset, rows_dst, 0).reshape(
        row_blocks, 128, HEADS, HEAD_DIM
    )
    self_rounded = lax.optimization_barrier(self_weight.astype(jnp.bfloat16))
    self_part = self_rounded.astype(jnp.float32).transpose(0, 2, 1)[..., None] * self_values.astype(
        jnp.float32
    )
    weighted = weighted + self_part.reshape(row_blocks, 128, feature_width)
    weighted_rows = weighted.reshape(rows_dst, feature_width)
    denominator_rows = denominator.transpose(1, 0, 2).reshape(HEADS, rows_dst)
    weighted_own, denominator_own = (
        lax.psum_scatter(
            weighted_rows.astype(jnp.bfloat16), "src", scatter_dimension=0, tiled=True
        ).astype(jnp.float32),
        lax.psum_scatter(
            denominator_rows.astype(jnp.bfloat16), "src", scatter_dimension=1, tiled=True
        ).astype(jnp.float32),
    )
    mixed_rows = weighted_own.reshape(own_rows, HEADS, HEAD_DIM) / denominator_own.T[:, :, None]
    result = jax.nn.elu(mixed_rows.reshape(own_rows, feature_width) + out_bias)
    return result.astype(jnp.bfloat16)


def solution(mesh):
    placed = (
        P(("src", "dst"), None),
        P(),
        P(),
        P(),
        P(),
        P("dst", "src", None, None),
        P("dst", "src", None, None, None),
        P("dst", "src"),
    )
    return jax.shard_map(
        on_device, mesh=mesh, in_specs=placed, out_specs=P(("dst", "src"), None), check_vma=False
    )
```

profile of v0, /device:TPU:8, one launch (start us, length us, event | category | flops | bytes accessed | tf_op | source)
XLA Modules:
  0.0 1036.6 jit_solution(7176538615227413374)
XLA Ops:
  7.4 0.9 copy-done
  8.3 1.9 bitcast_reduce_fusion.1
  10.2 52.3 %all_gather.7 = bf16[16,16384]{1,0:T(8,128)(2,1)S(1)} all-gather(bf16[16,512]{1,0:T(8,128)(2,1)S(1)} %maximum_bitcast_fusion), channel_id=1, replica_groups=mesh['dst'=32,'src'=8] {'dst'}, dimensions={1}, use_global_device_ids=true | all-gather | bytes 540672 | tf_op jit(solution)/shard_map/all_gather | solution.py:53
  64.1 61.0 %all-reduce.3.cloned.1.call-done = bf16[32,8,128]{2,1,0:T(8,128)(2,1)} async-done(((bf16[32,8,128]{2,1,0:T(8,128)(2,1)}), bf16[32,8,128]{2,1,0:T(8,128)(2,1)}) %all-reduce.3.cloned.1.call-update) | async-done | bytes 65552 | tf_op jit(solution)/shard_map/psum | solution.py:13
  125.1 0.8 transpose.75
  125.9 38.4 %while.22 = (s32[]{:T(128)}, f32[32,8,128]{2,1,0:T(8,128)S(1)}, s32[]{:T(128)}, s32[2,256]{1,0:T(2,128)S(1)}, s32[256,16,128]{2,1,0:T(8,128)}, /*index=5*/s32[]{...) while((s32[]{:T(128)}, f32[32,8,128]{2,1,0:T(8,128)S(1)}, ...), condition=%wide.region_6.7_spmd, body=%wide.region_3.6_spmd.sunk | while | flops 13633670 | bytes 2112275 | solution.py:101
  126.6 0.9 constant_dynamic-slice_fusion.8
  129.7 4.7 fusion.61
  134.4 1.1 scatter_fusion
  136.2 0.9 constant_dynamic-slice_fusion.8
  139.3 4.7 fusion.61
  144.0 1.1 scatter_fusion
  145.8 0.9 constant_dynamic-slice_fusion.8
  148.9 4.7 fusion.61
  153.6 1.1 scatter_fusion
  155.4 0.9 constant_dynamic-slice_fusion.8
  158.5 4.7 fusion.61
  163.2 1.1 scatter_fusion
  165.7 175.4 %all-reduce.5.cloned.1.call-done = bf16[32,8,128]{2,1,0:T(8,128)(2,1)} async-done(((bf16[32,8,128]{2,1,0:T(8,128)(2,1)}), bf16[32,8,128]{2,1,0:T(8,128)(2,1)}) %all-reduce.5.cloned.1.call-update) | async-done | bytes 65552 | tf_op jit(solution)/shard_map/pmax | solution.py:105
  341.1 1.5 convert_element_type.61
  342.6 38.5 %all-gather.2.cloned.1.call-done = bf16[16384,256]{0,1:T(8,128)(2,1)} async-done(((bf16[512,256]{0,1:T(8,128)(2,1)}), bf16[16384,256]{0,1:T(8,128)(2,1)}) %all-gather.2.cloned.1.call-update) | async-done | bytes 8388624 | tf_op jit(solution)/shard_map/all_gather | solution.py:52
  381.1 9.2 copy.53
  390.2 24.4 %copy.47 = bf16[128,128,8,32]{3,2,1,0:T(8,128)(2,1)} copy(bf16[128,128,8,32]{1,0,3,2:T(8,128)(2,1)} %bitcast.136) | data formatting | bytes 16777216 | tf_op jit(solution)/shard_map/while | solution.py:124
  414.6 2.4 broadcast_in_dim.36
  417.0 134.6 %while.23 = (s32[]{:T(128)}, f32[32,128,256]{2,1,0:T(8,128)}, f32[32,8,128]{2,1,0:T(8,128)S(1)}, s32[]{:T(128)}, s32[2,256]{1,0:T(2,128)S(1)}, /*index=5*/bf16[1...) while((s32[]{:T(128)}, f32[32,128,256]{2,1,0:T(8,128)}, ...), condition=%wide.region_12.13_spmd, body=%wide.region_8.12_spmd.sunk | while | flops 165152896 | bytes 18496492 | solution.py:124
  417.3 1.5 gather_fusion.3
  419.9 4.9 gather_fusion.2
  424.8 0.9 constant_dynamic-slice_fusion.9
  427.3 8.3 fusion.67
  435.6 1.9 copy.64
  437.5 4.5 scatter_fusion.1
  442.0 7.6 fusion.68
  449.7 1.1 scatter_fusion.2
  450.9 1.5 gather_fusion.3
  453.5 5.0 gather_fusion.2
  458.5 0.9 constant_dynamic-slice_fusion.9
  461.0 8.3 fusion.67
  469.2 1.9 copy.64
  471.2 4.6 scatter_fusion.1
  475.7 7.6 fusion.68
  483.4 1.1 scatter_fusion.2
  484.6 1.5 gather_fusion.3
  487.2 4.9 gather_fusion.2
  492.2 0.9 constant_dynamic-slice_fusion.9
  494.6 8.3 fusion.67
  502.9 1.9 copy.64
  504.8 4.4 scatter_fusion.1
  509.3 7.6 fusion.68
  516.9 1.1 scatter_fusion.2
  518.1 1.5 gather_fusion.3
  520.8 4.9 gather_fusion.2
  525.7 0.9 constant_dynamic-slice_fusion.9
  528.1 8.3 fusion.67
  536.4 1.9 copy.64
  538.3 4.5 scatter_fusion.1
  542.9 7.6 fusion.68
  550.5 1.1 scatter_fusion.2
  551.6 5.6 copy.49
  557.2 1.6 fusion.42
  558.9 3.6 fusion.35
  562.6 2.9 copy.50
  565.5 424.4 %reduce-scatter.5.cloned.1.call-done = bf16[8,512]{1,0:T(8,128)(2,1)} async-done(((bf16[8,4096]{1,0:T(8,128)(2,1)}), bf16[8,512]{1,0:T(8,128)(2,1)}) %reduce-scatter.5.cloned.1.call-update) | async-done | bytes 8208 | tf_op jit(solution)/shard_map/reduce_scatter | solution.py:141
  990.9 36.6 %reduce-scatter.3.cloned.1.call-done = bf16[512,256]{1,0:T(8,128)(2,1)} async-done(((bf16[4096,256]{1,0:T(8,128)(2,1)}), bf16[512,256]{1,0:T(8,128)(2,1)}) %reduce-scatter.3.cloned.1.call-update) | async-done | bytes 262160 | tf_op jit(solution)/shard_map/reduce_scatter | solution.py:138
  1027.5 1.9 fusion.37
  (124 shorter events, 25.3 us)
Async XLA Ops:
  7.4 0.9 copy-start
  7.4 118.6 %copy-start.5 = (s32[1,1,2,256]{3,2,1,0:T(2,128)S(1)}, s32[1,1,2,256]{3,2,1,0:T(2,128)}, u32[]{:S(2)}) copy-start(s32[1,1,2,256]{3,2,1,0:T(2,128)} %param.17) | copy-start | bytes 6148
  7.4 117.7 %all-reduce.3.cloned.1.call-start = ((), (), s32[]{:S(2)}) async-start(), calls=%async_computation.3 | async-start | bytes 131072 | tf_op jit(solution)/shard_map/psum | solution.py:13
  63.2 277.9 %all-reduce.5.cloned.1.call-start = ((), (), s32[]{:S(2)}) async-start(), calls=%async_computation.4 | async-start | bytes 131072 | tf_op jit(solution)/shard_map/pmax | solution.py:105
  64.1 100.3 %copy-start.2 = (f32[8,16384]{1,0:T(8,128)}, f32[8,16384]{1,0:T(8,128)S(1)}, u32[]{:S(2)}) copy-start(f32[8,16384]{1,0:T(8,128)S(1)} %slice.34) | copy-start | bytes 1572868
  125.9 38.4 %copy-start.3 = (bf16[32,8,128]{2,1,0:T(8,128)(2,1)S(1)}, bf16[32,8,128]{2,1,0:T(8,128)(2,1)}, u32[]{:S(2)}) copy-start(bf16[32,8,128]{2,1,0:T(8,128)(2,1)} %all-reduce.3.cloned.1.call-done) | copy-start | bytes 196612
  165.1 216.0 %all-gather.2.cloned.1.call-start = ((), (), s32[]{:S(2)}) async-start(), calls=%async_computation.2 | async-start | bytes 8650752 | tf_op jit(solution)/shard_map/all_gather | solution.py:52
  165.6 824.3 %reduce-scatter.5.cloned.1.call-start = ((), (), s32[]{:S(2)}) async-start(), calls=%async_computation.6 | async-start | bytes 73728 | tf_op jit(solution)/shard_map/reduce_scatter | solution.py:141
  551.6 5.6 copy-start.4
  558.9 468.6 %reduce-scatter.3.cloned.1.call-start = ((), (), s32[]{:S(2)}) async-start(), calls=%async_computation.5 | async-start | bytes 2359296 | tf_op jit(solution)/shard_map/reduce_scatter | solution.py:138
  558.9 470.5 %copy-start.1 = (bf16[512,128]{1,0:T(8,128)(2,1)S(1)}, bf16[512,128]{1,0:T(8,128)(2,1)}, u32[]{:S(2)}) copy-start(bf16[512,128]{1,0:T(8,128)(2,1)} %param.12) | copy-start | bytes 393220
  562.6 464.9 %copy-start.6 = (f32[256]{0:T(256)S(1)}, f32[256]{0:T(256)}, u32[]{:S(2)}) copy-start(f32[256]{0:T(256)} %param.16) | copy-start | bytes 3076
Sparse Core Ops, SparseCore 0:
  63.3 61.7 all-reduce.2
  165.2 175.8 all-reduce.4
  559.0 430.9 reduce-scatter.4
  992.5 34.9 reduce-scatter.2
Sparse Core Ops, SparseCore 1:
  168.0 213.0 all-gather.1
where the time goes:
time: 1040 us
  waiting for transfers between devices  736 us (71%)
  local copies, waits for them, and re-layouts  99.6 us (10%)
  other arithmetic  96.5 us (9%)
  blocking collectives  52.3 us (5%)
  matrix products  35 us (3%)
  between operations  15.4 us (1%)
    reduce_scatter x1, waiting for transfers between devices, on_device(): lax.psum_scatter(denominator_rows.astype(jnp.bfloat16), 'src', scatter_di...  424 us
    pmax x1, waiting for transfers between devices, on_device(): maxima = lax.pmax(maxima.astype(jnp.bfloat16), 'src').astype(maxima.dtype)  175 us
    psum x1, waiting for transfers between devices, from_root(): return lax.psum(block, axis)  61 us
    all_gather x1, blocking collectives, on_device(): lax.all_gather(terms_of(projected, source_att, target_att).astype(jnp.bfl...  52.3 us
    all_gather x1, waiting for transfers between devices, on_device(): lax.all_gather(projected.astype(jnp.bfloat16), 'dst', axis=0, tiled=True)  38.5 us
    reduce_scatter x1, waiting for transfers between devices, on_device(): lax.psum_scatter(weighted_rows.astype(jnp.bfloat16), 'src', scatter_dimen...  36.6 us
    dot_general x4, matrix products, sum_step(): jnp.einsum('ghab,gbhc->gahc', rounded, value_blocks[col_ids], preferred_e...  33.1 us
    reduce_sum x4, other arithmetic, sum_step(): denominator = denominator.at[row_ids].add(jnp.sum(weight, axis=3))  30.6 us
  transfers between devices with their start and end apart: 5, of which 5 were waited for; matrix products, arithmetic and copies ran while one was open for 1% of the time, Pallas kernels for 0%

commit v1 on v0

--- a/solution.py
+++ b/solution.py
@@ -10,7 +10,7 @@
 
 def from_root(block, axis, holder):
     block = jnp.where(lax.axis_index(axis) == holder, block, jnp.zeros_like(block))
-    return lax.psum(block, axis)
+    return jnp.sum(lax.all_gather(block, axis), axis=0)
 
 
 def leaky_relu(inputs):

time: 1040 us -> 990 us (0.952)
  waiting for transfers between devices: 736 us -> 675 us
  blocking collectives: 52.3 us -> 65.8 us
    psum x1 -> x0, waiting for transfers between devices: 61 us -> none  [from_root(): return lax.psum(block, axis)]
    all_gather x0 -> x1, blocking collectives: none -> 13.5 us  [from_root(): return jnp.sum(lax.all_gather(block, axis), axis=0)]
  transfers between devices with their start and end apart: 5 -> 4, of which waited for: 5 -> 4; matrix products, arithmetic and copies ran while one was open for 1% -> 1% of each run, Pallas kernels for 0% -> 0%
where the time goes in v1:
time: 990 us; the launch traced here: 987 us
  waiting for transfers between devices  675 us (68%)
  local copies, waits for them, and re-layouts  98.9 us (10%)
  other arithmetic  95.1 us (10%)
  blocking collectives  65.8 us (7%)
  matrix products  35 us (4%)
  between operations  15.5 us (2%)
    reduce_scatter x1, waiting for transfers between devices, on_device(): lax.psum_scatter(denominator_rows.astype(jnp.bfloat16), 'src', scatter_di...  424 us
    pmax x1, waiting for transfers between devices, on_device(): maxima = lax.pmax(maxima.astype(jnp.bfloat16), 'src').astype(maxima.dtype)  175 us
    all_gather x1, blocking collectives, on_device(): lax.all_gather(terms_of(projected, source_att, target_att).astype(jnp.bfl...  52.2 us
    all_gather x1, waiting for transfers between devices, on_device(): lax.all_gather(projected.astype(jnp.bfloat16), 'dst', axis=0, tiled=True)  38.8 us
    reduce_scatter x1, waiting for transfers between devices, on_device(): lax.psum_scatter(weighted_rows.astype(jnp.bfloat16), 'src', scatter_dimen...  36.6 us
    dot_general x4, matrix products, sum_step(): jnp.einsum('ghab,gbhc->gahc', rounded, value_blocks[col_ids], preferred_e...  33.1 us
    reduce_sum x4, other arithmetic, sum_step(): denominator = denominator.at[row_ids].add(jnp.sum(weight, axis=3))  30.6 us
    while x2, local copies, waits for them, and re-layouts, on_device(): weighted, denominator = lax.fori_loop(0, steps_live, sum_step, start_state)  30 us
  transfers between devices with their start and end apart: 4, of which 4 were waited for; matrix products, arithmetic and copies ran while one was open for 1% of the time, Pallas kernels for 0%

profile of v1, /device:TPU:8, one launch (start us, length us, event | category | flops | bytes accessed | tf_op | source)
XLA Modules:
  0.0 986.8 jit_solution(14529610667686618568)
XLA Ops:
  8.3 1.9 bitcast_reduce_fusion.2
  10.2 52.2 %all_gather.13 = bf16[16,16384]{1,0:T(8,128)(2,1)S(1)} all-gather(bf16[16,512]{1,0:T(8,128)(2,1)S(1)} %maximum_bitcast_fusion), channel_id=1, replica_groups=mesh['dst'=32,'src'=8] {'dst'}, dimensions={1}, use_global_device_ids=true | all-gather | bytes 540672 | tf_op jit(solution)/shard_map/all_gather | solution.py:53
  62.6 13.5 %all-gather = bf16[64,4096]{1,0:T(8,128)(2,1)S(1)} all-gather(bf16[8,4096]{1,0:T(8,128)(2,1)S(1)} %fusion.39), channel_id=2, replica_groups=mesh['dst'=32,'src'=8] {'src'}, dimensions={0}, use_global_device_ids=true | all-gather | bytes 589824 | tf_op jit(solution)/shard_map/all_gather | solution.py:13
  76.4 38.4 %while.22 = (s32[]{:T(128)}, f32[32,8,128]{2,1,0:T(8,128)S(1)}, s32[]{:T(128)}, s32[2,256]{1,0:T(2,128)S(1)}, s32[256,16,128]{2,1,0:T(8,128)}, /*index=5*/s32[]{...) while((s32[]{:T(128)}, f32[32,8,128]{2,1,0:T(8,128)S(1)}, ...), condition=%wide.region_6.7_spmd, body=%wide.region_3.6_spmd.sunk | while | flops 13633670 | bytes 2112275 | solution.py:101
  77.1 0.9 constant_dynamic-slice_fusion.8
  80.1 4.7 fusion.60
  84.9 1.1 scatter_fusion
  86.7 0.9 constant_dynamic-slice_fusion.8
  89.7 4.7 fusion.60
  94.5 1.1 scatter_fusion
  96.3 0.9 constant_dynamic-slice_fusion.8
  99.3 4.7 fusion.60
  104.1 1.1 scatter_fusion
  105.9 0.9 constant_dynamic-slice_fusion.8
  108.9 4.7 fusion.60
  113.7 1.1 scatter_fusion
  114.8 0.7 fusion.38
  116.1 175.0 %all-reduce.2.cloned.1.call-done = bf16[32,8,128]{2,1,0:T(8,128)(2,1)} async-done(((bf16[32,8,128]{2,1,0:T(8,128)(2,1)}), bf16[32,8,128]{2,1,0:T(8,128)(2,1)}) %all-reduce.2.cloned.1.call-update) | async-done | bytes 65552 | tf_op jit(solution)/shard_map/pmax | solution.py:105
  291.1 1.5 convert_element_type.68
  292.6 38.8 %all-gather.3.cloned.1.call-done = bf16[16384,256]{0,1:T(8,128)(2,1)} async-done(((bf16[512,256]{0,1:T(8,128)(2,1)}), bf16[16384,256]{0,1:T(8,128)(2,1)}) %all-gather.3.cloned.1.call-update) | async-done | bytes 8388624 | tf_op jit(solution)/shard_map/all_gather | solution.py:52
  331.4 9.2 copy.53
  340.5 24.4 %copy.47 = bf16[128,128,8,32]{3,2,1,0:T(8,128)(2,1)} copy(bf16[128,128,8,32]{1,0,3,2:T(8,128)(2,1)} %bitcast.155) | data formatting | bytes 16777216 | tf_op jit(solution)/shard_map/while | solution.py:124
  364.9 2.4 broadcast_in_dim.36
  367.3 134.6 %while.23 = (s32[]{:T(128)}, f32[32,128,256]{2,1,0:T(8,128)}, f32[32,8,128]{2,1,0:T(8,128)S(1)}, s32[]{:T(128)}, s32[2,256]{1,0:T(2,128)S(1)}, /*index=5*/bf16[1...) while((s32[]{:T(128)}, f32[32,128,256]{2,1,0:T(8,128)}, ...), condition=%wide.region_12.13_spmd, body=%wide.region_8.12_spmd.sunk | while | flops 165152896 | bytes 18496492 | solution.py:124
  367.6 1.5 gather_fusion.3
  370.3 4.9 gather_fusion.2
  375.1 0.9 constant_dynamic-slice_fusion.9
  377.6 8.3 fusion.66
  385.9 1.9 copy.64
  387.8 4.5 scatter_fusion.1
  392.3 7.6 fusion.67
  400.0 1.1 scatter_fusion.2
  401.2 1.5 gather_fusion.3
  403.8 5.0 gather_fusion.2
  408.8 0.9 constant_dynamic-slice_fusion.9
  411.3 8.3 fusion.66
  419.6 1.9 copy.64
  421.5 4.6 scatter_fusion.1
  426.1 7.6 fusion.67
  433.7 1.1 scatter_fusion.2
  434.9 1.5 gather_fusion.3
  437.6 4.9 gather_fusion.2
  442.5 0.9 constant_dynamic-slice_fusion.9
  444.9 8.3 fusion.66
  453.2 1.9 copy.64
  455.1 4.4 scatter_fusion.1
  459.6 7.6 fusion.67
  467.2 1.1 scatter_fusion.2
  468.5 1.5 gather_fusion.3
  471.1 4.9 gather_fusion.2
  476.0 0.9 constant_dynamic-slice_fusion.9
  478.4 8.3 fusion.66
  486.7 1.9 copy.64
  488.6 4.5 scatter_fusion.1
  493.2 7.6 fusion.67
  500.8 1.1 scatter_fusion.2
  501.9 5.6 copy.49
  507.6 1.6 fusion.41
  509.3 3.6 fusion.35
  512.9 2.9 copy.50
  515.8 424.4 %reduce-scatter.5.cloned.1.call-done = bf16[8,512]{1,0:T(8,128)(2,1)} async-done(((bf16[8,4096]{1,0:T(8,128)(2,1)}), bf16[8,512]{1,0:T(8,128)(2,1)}) %reduce-scatter.5.cloned.1.call-update) | async-done | bytes 8208 | tf_op jit(solution)/shard_map/reduce_scatter | solution.py:141
  940.3 0.7 convert_bitcast_fusion.3
  941.2 36.6 %reduce-scatter.3.cloned.1.call-done = bf16[512,256]{1,0:T(8,128)(2,1)} async-done(((bf16[4096,256]{1,0:T(8,128)(2,1)}), bf16[512,256]{1,0:T(8,128)(2,1)}) %reduce-scatter.3.cloned.1.call-update) | async-done | bytes 262160 | tf_op jit(solution)/shard_map/reduce_scatter | solution.py:138
  977.8 1.9 fusion.37
  (121 shorter events, 23.5 us)
Async XLA Ops:
  7.4 0.9 copy-start
  7.4 69.0 %copy-start.4 = (s32[1,1,2,256]{3,2,1,0:T(2,128)S(1)}, s32[1,1,2,256]{3,2,1,0:T(2,128)}, u32[]{:S(2)}) copy-start(s32[1,1,2,256]{3,2,1,0:T(2,128)} %param.17) | copy-start | bytes 6148
  7.4 283.7 %all-reduce.2.cloned.1.call-start = ((), (), s32[]{:S(2)}) async-start(), calls=%async_computation.3 | async-start | bytes 131072 | tf_op jit(solution)/shard_map/pmax | solution.py:105
  62.6 52.2 %copy-start.2 = (f32[8,16384]{1,0:T(8,128)}, f32[8,16384]{1,0:T(8,128)S(1)}, u32[]{:S(2)}) copy-start(f32[8,16384]{1,0:T(8,128)S(1)} %slice.34) | copy-start | bytes 1572868
  115.5 215.9 %all-gather.3.cloned.1.call-start = ((), (), s32[]{:S(2)}) async-start(), calls=%async_computation.2 | async-start | bytes 8650752 | tf_op jit(solution)/shard_map/all_gather | solution.py:52
  116.0 824.2 %reduce-scatter.5.cloned.1.call-start = ((), (), s32[]{:S(2)}) async-start(), calls=%async_computation.5 | async-start | bytes 73728 | tf_op jit(solution)/shard_map/reduce_scatter | solution.py:141
  501.9 5.6 copy-start.3
  509.2 468.6 %reduce-scatter.3.cloned.1.call-start = ((), (), s32[]{:S(2)}) async-start(), calls=%async_computation.4 | async-start | bytes 2359296 | tf_op jit(solution)/shard_map/reduce_scatter | solution.py:138
  509.2 470.5 %copy-start.1 = (bf16[512,128]{1,0:T(8,128)(2,1)S(1)}, bf16[512,128]{1,0:T(8,128)(2,1)}, u32[]{:S(2)}) copy-start(bf16[512,128]{1,0:T(8,128)(2,1)} %param.12) | copy-start | bytes 393220
  512.9 464.9 %copy-start.5 = (f32[256]{0:T(256)S(1)}, f32[256]{0:T(256)}, u32[]{:S(2)}) copy-start(f32[256]{0:T(256)} %param.16) | copy-start | bytes 3076
Sparse Core Ops, SparseCore 0:
  115.6 175.4 all-reduce.1
  509.3 430.9 reduce-scatter.4
  942.8 34.9 reduce-scatter.2
Sparse Core Ops, SparseCore 1:
  118.7 212.6 all-gather.2
